TPU v7x, 512 devices: a whole 4x8x8 slice. The times are simulated.
512 devices in a mesh: lat: 32 (over x, z), lev: 16 (over y, core).
Axes of the slice: x: 4, y: 8, z: 8, core: 2. Of those that a mesh axis runs over, the one named last changes fastest.
Arguments:
- fields: float32 [2, 128, 64, 3072], P(None, 'lat', 'lev'), may hold values from -6 to 6
- courant: bfloat16 [2, 128, 64, 3072], P(None, 'lat', 'lev'), may hold values from -0.3984375 to 0.3984375
- cutoffs: int32 [128], replicated, may hold values from 1 to 1536, as said below
- surface: float32 [128, 3072], P('lat'), may hold values from -6 to 6
- remap_weights: float32 [64, 64], replicated, may hold values from -0.25 to 0.75
Outputs:
- remapped: float32 [2, 128, 64, 3072], P(None, 'lat', None, 'lev')
- geopotential: float32 [128, 64, 3072], P('lat', None, 'lev')
Inputs may be any that keep to these rules, and one draw needn't show every extreme that they name: cutoffs[j] is 1536 except on the first and the last 16 latitudes, where it lies between 1 and 127; it equals 127 on some latitude among the first 16.
All inputs are finite; a program needn't handle non-finite values.
Results may differ from a plain program's by a relative error of at most 0.0003.
Values may be sent and summed in bfloat16 or wider, within the bound.
A program may use at most 64 MiB of HBM per device.

v0:
```python
import math
import jax
import jax.numpy as jnp
from jax import lax
from jax.sharding import PartitionSpec as P

KMAX = 128


def with_halo(shard, sides, width):
    for axis, dim in sides:
        size, length = (lax.axis_size(axis), shard.shape[dim])
        up = [(i, (i + 1) % size) for i in range(size - 1)]
        down = [(j, i) for i, j in up]
        last = lax.slice_in_dim(shard, length - width, length, axis=dim)
        leading = lax.slice_in_dim(shard, 0, width, axis=dim)
        before = lax.ppermute(last, axis, up)
        after = lax.ppermute(leading, axis, down)
        shard = jnp.concatenate([before, shard, after], axis=dim)
    return shard


def entering(part, axis, combine, identity):
    count = lax.axis_size(axis)
    place = lax.axis_index(axis)
    ahead = count - 1 - place
    gathered = lax.all_gather(part, axis)
    state = jnp.zeros_like(part) + jnp.asarray(identity, part.dtype)

    def one(lap, state):
        source = count - 1 - lap
        return combine(state, lax.dynamic_index_in_dim(gathered, source, 0, False))

    return lax.fori_loop(0, ahead, one, state)


def lon_part(values, east_wind):
    interface = (
        7.0 * (values + jnp.roll(values, -1, -1))
        - (jnp.roll(values, 1, -1) + jnp.roll(values, -2, -1))
    ) / 12.0
    face_wind = 0.5 * (east_wind + jnp.roll(east_wind, -1, -1))
    flux_faces = face_wind * interface
    return flux_faces - jnp.roll(flux_faces, 1, -1)


def lat_part(padded, north_wind):
    row_count = padded.shape[1] - 4
    interface = (
        7.0 * (padded[:, 1 : row_count + 2] + padded[:, 2 : row_count + 3])
        - (padded[:, 0 : row_count + 1] + padded[:, 3 : row_count + 4])
    ) / 12.0
    face_wind = 0.5 * (north_wind[0 : row_count + 1] + north_wind[1 : row_count + 2])
    flux_faces = face_wind * interface
    return flux_faces[:, 1:] - flux_faces[:, :-1]


def advance(padded, east_wind, north_wind):
    middle = padded[:, 2:-2]
    return middle - lon_part(middle, east_wind) - lat_part(padded, north_wind)


def spectral_tables(length, wave_count):
    wave_numbers = jnp.arange(wave_count, dtype=jnp.int32)
    points = jnp.arange(length, dtype=jnp.int32)
    phase = points[:, None] * wave_numbers[None, :] % length
    angle = phase.astype(jnp.float32) * (2.0 * math.pi / length)
    return (jnp.cos(angle), jnp.sin(angle))


def polar_filter(values, cutoff_rows, cosine_table, sine_table):
    length = values.shape[-1]
    wave_count = cosine_table.shape[1]
    flagged = cutoff_rows < length // 2

    def smooth(inputs):
        real_part = jnp.einsum(
            "frln,nk->frlk", inputs, cosine_table, precision=lax.Precision.HIGHEST
        )
        imag_part = jnp.einsum("frln,nk->frlk", inputs, sine_table, precision=lax.Precision.HIGHEST)
        wave_numbers = jnp.arange(wave_count, dtype=jnp.int32)
        doubled = jnp.where(wave_numbers == 0, 1.0, 2.0).astype(jnp.float32)
        weight = (
            jnp.where(wave_numbers[None, :] <= cutoff_rows[:, None], doubled[None, :], 0.0) / length
        )
        weight = weight[None, :, None, :]
        lowpass = jnp.einsum(
            "frlk,nk->frln", real_part * weight, cosine_table, precision=lax.Precision.HIGHEST
        )
        lowpass = lowpass + jnp.einsum(
            "frlk,nk->frln", imag_part * weight, sine_table, precision=lax.Precision.HIGHEST
        )
        return jnp.where(flagged[None, :, None, None], lowpass, inputs)

    return lax.cond(jnp.any(flagged), smooth, lambda inputs: inputs, values)


def upward_matrix(count):
    levels = jnp.arange(count, dtype=jnp.int32)
    deeper = (levels[None, :] > levels[:, None]).astype(jnp.float32)
    same_level = (levels[None, :] == levels[:, None]).astype(jnp.float32)
    return deeper + 0.5 * same_level


def shards(fields, courant, cutoffs, surface, remap_weights):
    band_rows = fields.shape[1]
    length = fields.shape[-1]
    nyquist = length // 2
    first_row = lax.axis_index("lat") * band_rows
    padded_cut = jnp.pad(cutoffs, 2, constant_values=nyquist)
    own_cut = lax.dynamic_slice_in_dim(padded_cut, first_row + 2, band_rows)
    cosine_table, sine_table = spectral_tables(length, KMAX)
    rim_depth = 1
    winds_rimmed = with_halo(courant, (("lat", 1),), rim_depth).astype(jnp.float32)
    east_wind = winds_rimmed[0, 1:-1]
    north_wind = winds_rimmed[1]
    transported = fields
    for repeat in range(2):
        padded = with_halo(transported, (("lat", 1),), 2)
        transported = polar_filter(
            advance(padded, east_wind, north_wind), own_cut, cosine_table, sine_table
        )
    level_count = remap_weights.shape[0]
    geo_scale = level_count ** (-0.5)
    heat_rows = transported[1]
    own_total = jnp.sum(heat_rows, axis=1)
    deeper = entering(
        own_total, "lev", lambda earlier, later: earlier + later, jnp.zeros_like(own_total)
    )
    within = jnp.einsum(
        "kl,jln->jkn", upward_matrix(heat_rows.shape[1]), heat_rows, precision=lax.Precision.HIGHEST
    )
    geo_levels = surface[:, None, :] + geo_scale * (deeper[:, None, :] + within)
    packed = jnp.concatenate([transported, geo_levels[None]], axis=0)
    columns = lax.all_to_all(packed, "lev", split_axis=3, concat_axis=2, tiled=True)
    column_columns = columns[:2]
    remapped = jnp.einsum(
        "pk,fjkn->fjpn", remap_weights, column_columns, precision=lax.Precision.HIGHEST
    )
    geo_columns = columns[2:3]
    geopotential = geo_columns[0]
    return (remapped, geopotential)


def solution(mesh):
    return jax.shard_map(
        shards,
        mesh=mesh,
        in_specs=(
            P(None, "lat", "lev", None),
            P(None, "lat", "lev", None),
            P(),
            P("lat", None),
            P(),
        ),
        out_specs=(P(None, "lat", None, "lev"), P("lat", None, "lev")),
        check_vma=False,
    )
```

profile of v0, /device:TPU:1, one launch (start us, length us, event | category | flops | bytes accessed | tf_op | source)
XLA Modules:
  0.0 197.7 jit_solution(3813942538770517226)
XLA Ops:
  0.6 0.0 copy-start
  0.6 0.0 copy-start.3
  0.7 0.9 fusion.80
  1.6 4.8 %collective-permute-start = (bf16[2,1,4,3072]{3,2,1,0:T(4,128)(2,1)S(1)}, bf16[2,1,4,3072]{3,2,1,0:T(4,128)(2,1)S(1)}, u32[]{:S(2)}, u32[]{:S(2)}) collective-permute-start(bf16[2,1,4,3072]{3,2,1,0:T(4,128)(2,1)S(1)} %get-tuple-element.130), channel_id=1, source_target_pairs={{0,16},{16,32},{32,48},{48,64},{64,80},{80,96},{96,112},{112,128},... | collective-permute-start | bytes 147464 | tf_op jit(solution)/shard_map/ppermute | solution.py:17
  6.4 1.3 collective-permute-start.1
  7.7 1.8 fusion.79
  9.5 5.3 %collective-permute-start.2 = (f32[2,2,4,3072]{3,2,1,0:T(4,128)}, f32[2,2,4,3072]{3,2,1,0:T(4,128)}, u32[]{:S(2)}, u32[]{:S(2)}) collective-permute-start(f32[2,2,4,3072]{3,2,1,0:T(4,128)} %get-tuple-element.128), channel_id=1, source_target_pairs={{0,16},{16,32},{32,48},{48,64},{64,80},{80,96},{96,112},{112,128},... | collective-permute-start | bytes 589832 | tf_op jit(solution)/shard_map/ppermute | solution.py:17
  14.8 1.3 collective-permute-start.3
  16.1 0.8 fusion.77
  16.9 1.0 fusion.78
  17.9 7.2 %fusion.35 = (f32[3072,128]{1,0:T(8,128)S(1)}, f32[3072,128]{1,0:T(8,128)}) fusion(), kind=kLoop, calls=%fused_computation.39 | loop fusion | flops 3538944 | bytes 3145728 | tf_op jit(solution)/shard_map/sin | solution.py:68
  25.1 0.1 broadcast_compare_fusion
  25.2 0.7 fusion.73
  25.9 0.3 slice.159
  26.8 0.0 slice-start
  26.8 0.0 copy-start.4
  26.8 0.2 maximum_convert_fusion
  27.0 0.2 slice_bitcast_fusion
  27.2 0.1 fusion.59
  27.3 0.1 fusion.61
  27.4 0.9 constant_dynamic-update-slice_fusion.1
  28.4 0.4 fusion.52
  28.8 0.1 slice.201
  28.9 0.2 fusion.46
  29.1 0.3 fusion.49
  29.4 6.1 %conditional.2 = (f32[2,4,4,3072]{3,2,1,0:T(4,128)S(1)}) conditional(s32[]{:T(128)} %convert_element_type.28, f32[2,4,4,3072]{3,2,1,0:T(4,128)S(1)} %fusion.49, (pred[4]{0:T(512)(128)(4,1)S(1)}, f32[2,4,4,3072]{3,2,1,0:T(4,128)S(1)}, f32[3072,128]{1,0:T(8,128)}, s32[4]{0:T(128)S(1)}, f32[3072,128]{1,0:T(8,128)}, /*index=5*/f32[3072,128]{1,0:T(8,128)S(1)}, ...), branch_computations={%region_1.2_spmd, %region_2.3_spmd} | conditional | flops 604186368 | bytes 15014968 | solution.py:95
  29.5 0.1 select_multiply_fusion
  29.6 1.1 fusion.11
  30.7 0.2 copy-done.1
  30.9 1.1 fusion.8
  32.0 1.7 fusion.4
  33.7 1.8 fusion
  35.5 0.1 fusion.74
  35.6 0.3 slice.215
  35.9 0.3 fusion.75
  36.2 4.0 %collective-permute-start.4 = (f32[2,2,4,3072]{3,2,1,0:T(4,128)S(1)}, f32[2,2,4,3072]{3,2,1,0:T(4,128)S(1)}, u32[]{:S(2)}, u32[]{:S(2)}) collective-permute-start(f32[2,2,4,3072]{3,2,1,0:T(4,128)S(1)} %get-tuple-element.119), channel_id=1, source_target_pairs={{0,16},{16,32},{32,48},{48,64},{64,80},{80,96},{96,112},{112,128},... | collective-permute-start | bytes 589832 | tf_op jit(solution)/shard_map/ppermute | solution.py:17
  40.2 1.3 collective-permute-start.5
  41.5 0.4 fusion.56
  41.9 0.1 slice.217
  41.9 0.8 collective-permute-done.4
  42.8 5.6 %collective-permute-done.5 = f32[2,2,4,3072]{3,2,1,0:T(4,128)S(1)} collective-permute-done((f32[2,2,4,3072]{3,2,1,0:T(4,128)S(1)}, f32[2,2,4,3072]{3,2,1,0:T(4,128)S(1)}, u32[]{:S(2)}, u32[]{:S(2)}) %collective-permute-start.5) | collective-permute-done | bytes 196640 | tf_op jit(solution)/shard_map/ppermute | solution.py:18
  48.4 0.2 fusion.42
  48.6 1.0 fusion.48
  49.7 9.6 %conditional.3 = (f32[2,4,4,3072]{3,2,1,0:T(4,128)}) conditional(s32[]{:T(128)} %convert_element_type.28, f32[2,4,4,3072]{3,2,1,0:T(4,128)} %fusion.48, (pred[4]{0:T(512)(128)(4,1)S(1)}, f32[2,4,4,3072]{3,2,1,0:T(4,128)}, f32[3072,128]{1,0:T(8,128)}, s32[4]{0:T(128)S(1)}, f32[3072,128]{1,0:T(8,128)}, /*index=5*/f32[3072,128]{1,0:T(8,128)S(1)}, ...), branch_computations={%region_3.4_spmd, %region_4.5_spmd} | conditional | flops 604186368 | bytes 15014968 | solution.py:95
  49.7 0.1 select_multiply_fusion.1
  49.8 2.2 %fusion.25 = f32[2,4,4,128]{3,2,1,0:T(4,128)S(1)} fusion(f32[2,4,4,3072]{3,2,1,0:T(4,128)} %get-tuple-element.89, f32[3072,128]{1,0:T(8,128)S(1)} %get-tuple-element.94, f32[4,128]{1,0:T(4,128)S(1)} %select_multiply_fusion.1), kind=kOutput, calls=%fused_computation.24 | convolution fusion | flops 150999040 | bytes 1984512 | tf_op jit(solution)/shard_map/cond/branch_1_fun/frln,nk->frlk/dot_general | solution.py:80
  52.0 2.1 %fusion.22 = f32[2,4,4,128]{3,2,1,0:T(4,128)S(1)} fusion(f32[2,4,4,3072]{3,2,1,0:T(4,128)} %get-tuple-element.89, f32[3072,128]{1,0:T(8,128)S(1)} %copy-done.2, f32[4,128]{1,0:T(4,128)S(1)} %select_multiply_fusion.1), kind=kOutput, calls=%fused_computation.23 | convolution fusion | flops 150999040 | bytes 1984512 | tf_op jit(solution)/shard_map/cond/branch_1_fun/frln,nk->frlk/dot_general | solution.py:77
  54.1 1.7 fusion.18
  55.8 3.5 %fusion.14 = f32[2,4,4,3072]{3,2,1,0:T(4,128)} fusion(f32[2,4,4,3072]{3,2,1,0:T(4,128)} %get-tuple-element.89, f32[2,4,4,3072]{3,2,1,0:T(4,128)S(1)} %fusion.18, f32[2,4,4,128]{3,2,1,0:T(4,128)S(1)} %fusion.25, f32[3072,128]{1,0:T(8,128)S(1)} %get-tuple-element.94, pred[4]{0:T(512)(128)(4,1)S(1)} %get-tuple-element.88), kind=kOutput, calls=%fused_computation.15 | convolution fusion | flops 151191552 | bytes 2768900 | tf_op jit(solution)/shard_map/cond/branch_1_fun/frlk,nk->frln/dot_general | solution.py:90
  59.3 1.0 slice_reduce_fusion
  60.3 22.4 %all-gather.1 = f32[16,4,3072]{2,1,0:T(4,128)S(1)} all-gather(f32[1,4,3072]{2,1,0:T(4,128)S(1)} %bitcast.101), channel_id=2, replica_groups=mesh['lat'=32,'lev'=16] {'lev'}, dimensions={0}, use_global_device_ids=true | all-gather | bytes 835584 | tf_op jit(solution)/shard_map/all_gather | solution.py:27
  82.7 0.7 while.12
  83.5 1.4 fusion.30
  84.9 1.1 pad_maximum_fusion
  86.0 12.7 %copy.16 = f32[3,4,4,3072]{2,1,0,3:T(4,128)} copy(f32[3,4,4,3072]{3,2,1,0:T(4,128)S(1)} %pad_maximum_fusion) | data formatting | bytes 1179648 | tf_op jit(solution)/shard_map/concatenate | solution.py:134
  98.7 24.5 %reshape.111 = f32[16,1,9216]{2,1,0:T(1,128)S(1)} reshape(f32[3072,3,4,4]{3,2,1,0:T(4,128)} %bitcast.95) | data formatting | bytes 1179648
  123.2 22.8 %all_to_all.15 = f32[16,1,9216]{2,1,0:T(1,128)S(1)} all-to-all(f32[16,1,9216]{2,1,0:T(1,128)S(1)} %reshape.111), channel_id=1, replica_groups=mesh['lat'=32,'lev'=16] {'lev'}, dimensions={0} | all-to-all | bytes 1179648 | tf_op jit(solution)/shard_map/all_to_all | solution.py:135
  146.0 0.5 broadcast.173
  146.5 2.0 %reduce.1 = f32[16,9216]{1,0:T(8,128)S(1)} reduce(f32[16,1,9216]{2,1,0:T(1,128)S(1)} %all_to_all.15, f32[]{:T(128)} %broadcast.173), dimensions={1}, to_apply=%all_to_all.11.reduce_sub_computation | reduce | bytes 1179652 | tf_op jit(solution)/shard_map/all_to_all | solution.py:135
  148.6 31.6 %reshape.112 = f32[3072,3,4,4]{3,2,1,0:T(4,128)} reshape(f32[16,9216]{1,0:T(8,128)S(1)} %reduce.1) | data formatting | bytes 1179648
  180.2 15.1 %copy.17 = f32[3,4,4,16,192]{4,2,3,1,0:T(4,128)S(1)} copy(f32[3,4,4,16,192]{2,1,0,4,3:T(4,128)} %bitcast.96) | data formatting | bytes 1179648 | tf_op jit(solution)/shard_map/all_to_all | solution.py:135
  195.3 0.2 slice.196
  195.5 0.8 squeeze.19
  196.3 1.4 convolution_bitcast_fusion
  (41 shorter events, 0.5 us)
Async XLA Ops:
  0.6 195.7 %copy-start = (f32[64,64]{1,0:T(8,128)S(1)}, f32[64,64]{1,0:T(8,128)}, u32[]{:S(2)}) copy-start(f32[64,64]{1,0:T(8,128)} %param.15) | copy-start | bytes 49156
  0.6 16.3 %copy-start.3 = (f32[2,4,4,3072]{3,2,1,0:T(4,128)S(1)}, f32[2,4,4,3072]{3,2,1,0:T(4,128)}, u32[]{:S(2)}) copy-start(f32[2,4,4,3072]{3,2,1,0:T(4,128)} %param.11) | copy-start | bytes 1179652
  1.6 25.2 %collective-permute-start = (bf16[2,1,4,3072]{3,2,1,0:T(4,128)(2,1)S(1)}, bf16[2,1,4,3072]{3,2,1,0:T(4,128)(2,1)S(1)}, u32[]{:S(2)}, u32[]{:S(2)}) collective-permute-start(bf16[2,1,4,3072]{3,2,1,0:T(4,128)(2,1)S(1)} %get-tuple-element.130), channel_id=1, source_target_pairs={{0,16},{16,32},{32,48},{48,64},{64,80},{80,96},{96,112},{112,128},... | collective-permute-start | bytes 147464 | tf_op jit(solution)/shard_map/ppermute | solution.py:17
  6.4 20.4 %collective-permute-start.1 = (bf16[2,1,4,3072]{3,2,1,0:T(4,128)(2,1)S(1)}, bf16[2,1,4,3072]{3,2,1,0:T(4,128)(2,1)S(1)}, u32[]{:S(2)}, u32[]{:S(2)}) collective-permute-start(bf16[2,1,4,3072]{3,2,1,0:T(4,128)(2,1)S(1)} %get-tuple-element.131), channel_id=1, source_target_pairs={{16,0},{32,16},{48,32},{64,48},{80,64},{96,80},{112,96},{128,112},... | collective-permute-start | bytes 147464 | tf_op jit(solution)/shard_map/ppermute | solution.py:18
  9.5 17.9 %collective-permute-start.2 = (f32[2,2,4,3072]{3,2,1,0:T(4,128)}, f32[2,2,4,3072]{3,2,1,0:T(4,128)}, u32[]{:S(2)}, u32[]{:S(2)}) collective-permute-start(f32[2,2,4,3072]{3,2,1,0:T(4,128)} %get-tuple-element.128), channel_id=1, source_target_pairs={{0,16},{16,32},{32,48},{48,64},{64,80},{80,96},{96,112},{112,128},... | collective-permute-start | bytes 589832 | tf_op jit(solution)/shard_map/ppermute | solution.py:17
  14.8 14.1 %collective-permute-start.3 = (f32[2,2,4,3072]{3,2,1,0:T(4,128)}, f32[2,2,4,3072]{3,2,1,0:T(4,128)S(1)}, u32[]{:S(2)}, u32[]{:S(2)}) collective-permute-start(f32[2,2,4,3072]{3,2,1,0:T(4,128)} %get-tuple-element.129), channel_id=1, source_target_pairs={{16,0},{32,16},{48,32},{64,48},{80,64},{96,80},{112,96},{128,112},... | collective-permute-start | bytes 589832 | tf_op jit(solution)/shard_map/ppermute | solution.py:18
  17.9 7.2 %copy-start.7 = (s32[128]{0:T(128)S(1)}, s32[128]{0:T(128)}, u32[]{:S(2)}) copy-start(s32[128]{0:T(128)} %param.13) | copy-start | bytes 1540
  17.9 8.9 %copy-start.5 = (bf16[2,4,4,3072]{3,2,1,0:T(4,128)(2,1)S(1)}, bf16[2,4,4,3072]{3,2,1,0:T(4,128)(2,1)}, u32[]{:S(2)}) copy-start(bf16[2,4,4,3072]{3,2,1,0:T(4,128)(2,1)} %param.12) | copy-start | bytes 589828
  26.8 1.6 slice-start
  26.8 1.6 copy-start.4
  29.5 1.4 copy-start.1
  36.2 6.6 %collective-permute-start.4 = (f32[2,2,4,3072]{3,2,1,0:T(4,128)S(1)}, f32[2,2,4,3072]{3,2,1,0:T(4,128)S(1)}, u32[]{:S(2)}, u32[]{:S(2)}) collective-permute-start(f32[2,2,4,3072]{3,2,1,0:T(4,128)S(1)} %get-tuple-element.119), channel_id=1, source_target_pairs={{0,16},{16,32},{32,48},{48,64},{64,80},{80,96},{96,112},{112,128},... | collective-permute-start | bytes 589832 | tf_op jit(solution)/shard_map/ppermute | solution.py:17
  40.2 8.2 %collective-permute-start.5 = (f32[2,2,4,3072]{3,2,1,0:T(4,128)S(1)}, f32[2,2,4,3072]{3,2,1,0:T(4,128)S(1)}, u32[]{:S(2)}, u32[]{:S(2)}) collective-permute-start(f32[2,2,4,3072]{3,2,1,0:T(4,128)S(1)} %get-tuple-element.120), channel_id=1, source_target_pairs={{16,0},{32,16},{48,32},{64,48},{80,64},{96,80},{112,96},{128,112},... | collective-permute-start | bytes 589832 | tf_op jit(solution)/shard_map/ppermute | solution.py:18
  49.7 2.3 %copy-start.2 = (f32[3072,128]{1,0:T(8,128)S(1)}, f32[3072,128]{1,0:T(8,128)}, u32[]{:S(2)}) copy-start(f32[3072,128]{1,0:T(8,128)} %get-tuple-element.92) | copy-start | bytes 4718596 | tf_op jit(solution)/shard_map/cond
  59.3 24.2 %copy-start.6 = (f32[4,3072]{1,0:T(4,128)S(1)}, f32[4,3072]{1,0:T(4,128)}, u32[]{:S(2)}) copy-start(f32[4,3072]{1,0:T(4,128)} %param.14) | copy-start | bytes 147460
where the time goes:
time: 199 us; the launch traced here: 198 us
  local copies, waits for them, and re-layouts  92.4 us (46%)
  blocking collectives  45.2 us (23%)
  matrix products  18.1 us (9%)
  starting transfers between devices  18 us (9%)
  other arithmetic  15.6 us (8%)
  waiting for transfers between devices  6.48 us (3%)
    unnamed x15, local copies, waits for them, and re-layouts  57.1 us
    all_to_all x1, blocking collectives, shards(): lax.all_to_all(packed, 'lev', split_axis=3, concat_axis=2, tiled=True)  22.8 us
    all_gather x1, blocking collectives, entering(): gathered = lax.all_gather(part, axis)  22.4 us
    all_to_all x2, local copies, waits for them, and re-layouts, shards(): lax.all_to_all(packed, 'lev', split_axis=3, concat_axis=2, tiled=True)  15.6 us
    ppermute x3, starting transfers between devices, with_halo(): before = lax.ppermute(last, axis, up)  14.1 us
    concatenate x1, local copies, waits for them, and re-layouts, shards(): packed = jnp.concatenate([transported, geo_levels[None]], axis=0)  12.7 us
    sin x1, other arithmetic, spectral_tables(): return (jnp.cos(angle), jnp.sin(angle))  7.19 us
    ppermute x3, waiting for transfers between devices, with_halo(): after = lax.ppermute(leading, axis, down)  5.64 us
  transfers between devices with their start and end apart: 6, of which 2 were waited for; matrix products, arithmetic and copies ran while one was open for 7% of the time, Pallas kernels for 0%

commit v1 on v0

--- a/solution.py
+++ b/solution.py
@@ -1,3 +1,4 @@
+import functools
 import math
 import jax
 import jax.numpy as jnp
@@ -5,6 +6,22 @@
 from jax.sharding import PartitionSpec as P
 
 KMAX = 128
+
+
+def recover_cycles(mine_x, dev_axis, which_dim, k_dim):
+    wide_out = jnp.concatenate(
+        lax.all_to_all(
+            jnp.stack(jnp.split(mine_x, lax.psum(1, axis_name=dev_axis), which_dim), 0),
+            axis_name=dev_axis,
+            split_axis=0,
+            concat_axis=0,
+        ),
+        k_dim,
+    )
+    return wide_out
+
+
+pass_leaf_up = functools.partial(recover_cycles, dev_axis="lev", which_dim=3, k_dim=2)
 
 
 def with_halo(shard, sides, width):
@@ -132,7 +149,7 @@
     )
     geo_levels = surface[:, None, :] + geo_scale * (deeper[:, None, :] + within)
     packed = jnp.concatenate([transported, geo_levels[None]], axis=0)
-    columns = lax.all_to_all(packed, "lev", split_axis=3, concat_axis=2, tiled=True)
+    columns = pass_leaf_up(packed)
     column_columns = columns[:2]
     remapped = jnp.einsum(
         "pk,fjkn->fjpn", remap_weights, column_columns, precision=lax.Precision.HIGHEST

time: 199 us -> 113 us (0.57)
  local copies, waits for them, and re-layouts: 92.4 us -> 8.27 us
  other arithmetic: 15.6 us -> 11.7 us
  blocking collectives: 45.2 us -> 49.1 us
    unnamed x15 -> x13, local copies, waits for them, and re-layouts: 57.1 us -> 0.97 us
    all_to_all x2 -> x0, local copies, waits for them, and re-layouts: 15.6 us -> none  [shards(): lax.all_to_all(packed, 'lev', split_axis=3, concat_axis=2, tiled=True)]
    concatenate x1 -> x0, local copies, waits for them, and re-layouts: 12.7 us -> none  [shards(): packed = jnp.concatenate([transported, geo_levels[None]], axis=0)]
    all_to_all x1, blocking collectives: 22.8 us -> 26.7 us  [recover_cycles(): lax.all_to_all(jnp.stack(jnp.split(mine_x, lax.psum(1, axis_name=dev_axis...]
    all_to_all x1 -> x0, other arithmetic: 2.04 us -> none  [shards(): lax.all_to_all(packed, 'lev', split_axis=3, concat_axis=2, tiled=True)]
    dot_general x2, matrix products: 3.25 us -> 5.26 us  [smooth(): jnp.einsum('frln,nk->frlk', inputs, cosine_table, precision=lax.Precision...]
  transfers between devices with their start and end apart: 6 -> 6, of which waited for: 2 -> 2; matrix products, arithmetic and copies ran while one was open for 7% -> 13% of each run, Pallas kernels for 0% -> 0%
where the time goes in v1:
time: 113 us; the launch traced here: 112 us
  blocking collectives  49.1 us (43%)
  starting transfers between devices  18 us (16%)
  matrix products  16.4 us (15%)
  other arithmetic  11.7 us (10%)
  local copies, waits for them, and re-layouts  8.27 us (7%)
  waiting for transfers between devices  6.48 us (6%)
  between operations  1.75 us (2%)
    all_to_all x1, blocking collectives, recover_cycles(): lax.all_to_all(jnp.stack(jnp.split(mine_x, lax.psum(1, axis_name=dev_axis...  26.7 us
    all_gather x1, blocking collectives, entering(): gathered = lax.all_gather(part, axis)  22.4 us
    ppermute x3, starting transfers between devices, with_halo(): before = lax.ppermute(last, axis, up)  14.1 us
    sin x1, other arithmetic, spectral_tables(): return (jnp.cos(angle), jnp.sin(angle))  7.2 us
    ppermute x3, waiting for transfers between devices, with_halo(): after = lax.ppermute(leading, axis, down)  5.64 us
    dot_general x2, matrix products, smooth(): jnp.einsum('frln,nk->frlk', inputs, cosine_table, precision=lax.Precision...  5.26 us
    ppermute x3, starting transfers between devices, with_halo(): after = lax.ppermute(leading, axis, down)  3.86 us
    dot_general x2, matrix products, smooth(): jnp.einsum('frlk,nk->frln', imag_part * weight, sine_table, precision=lax...  3.63 us
  transfers between devices with their start and end apart: 6, of which 2 were waited for; matrix products, arithmetic and copies ran while one was open for 13% of the time, Pallas kernels for 0%

profile of v1, /device:TPU:1, one launch (start us, length us, event | category | flops | bytes accessed | tf_op | source)
XLA Modules:
  0.0 112.4 jit_solution(13110372620379916036)
XLA Ops:
  0.6 0.0 copy-start
  0.6 0.0 copy-start.3
  0.7 0.9 fusion.97
  1.6 4.8 %collective-permute-start = (bf16[2,1,4,3072]{3,2,1,0:T(4,128)(2,1)S(1)}, bf16[2,1,4,3072]{3,2,1,0:T(4,128)(2,1)S(1)}, u32[]{:S(2)}, u32[]{:S(2)}) collective-permute-start(bf16[2,1,4,3072]{3,2,1,0:T(4,128)(2,1)S(1)} %get-tuple-element.130), channel_id=1, source_target_pairs={{0,16},{16,32},{32,48},{48,64},{64,80},{80,96},{96,112},{112,128},... | collective-permute-start | bytes 147464 | tf_op jit(solution)/shard_map/ppermute | solution.py:34
  6.4 1.3 %collective-permute-start.1 = (bf16[2,1,4,3072]{3,2,1,0:T(4,128)(2,1)S(1)}, bf16[2,1,4,3072]{3,2,1,0:T(4,128)(2,1)S(1)}, u32[]{:S(2)}, u32[]{:S(2)}) collective-permute-start(bf16[2,1,4,3072]{3,2,1,0:T(4,128)(2,1)S(1)} %get-tuple-element.131), channel_id=1, source_target_pairs={{16,0},{32,16},{48,32},{64,48},{80,64},{96,80},{112,96},{128,112},... | collective-permute-start | bytes 147464 | tf_op jit(solution)/shard_map/ppermute | solution.py:35
  7.7 1.8 %fusion.96 = (f32[2,2,4,3072]{3,2,1,0:T(4,128)}, f32[2,2,4,3072]{3,2,1,0:T(4,128)}) fusion(f32[2,4,4,3072]{3,2,1,0:T(4,128)} %param.11), kind=kLoop, calls=%fused_computation.178 | loop fusion | bytes 786432 | tf_op jit(solution)/shard_map/slice | solution.py:32
  9.5 5.3 %collective-permute-start.2 = (f32[2,2,4,3072]{3,2,1,0:T(4,128)}, f32[2,2,4,3072]{3,2,1,0:T(4,128)}, u32[]{:S(2)}, u32[]{:S(2)}) collective-permute-start(f32[2,2,4,3072]{3,2,1,0:T(4,128)} %get-tuple-element.128), channel_id=1, source_target_pairs={{0,16},{16,32},{32,48},{48,64},{64,80},{80,96},{96,112},{112,128},... | collective-permute-start | bytes 589832 | tf_op jit(solution)/shard_map/ppermute | solution.py:34
  14.8 1.3 %collective-permute-start.3 = (f32[2,2,4,3072]{3,2,1,0:T(4,128)}, f32[2,2,4,3072]{3,2,1,0:T(4,128)S(1)}, u32[]{:S(2)}, u32[]{:S(2)}) collective-permute-start(f32[2,2,4,3072]{3,2,1,0:T(4,128)} %get-tuple-element.129), channel_id=1, source_target_pairs={{16,0},{32,16},{48,32},{64,48},{80,64},{96,80},{112,96},{128,112},... | collective-permute-start | bytes 589832 | tf_op jit(solution)/shard_map/ppermute | solution.py:35
  16.1 2.1 %fusion.95 = (f32[2,4,4,3071]{3,2,1,0:T(4,128)S(1)}, f32[2,4,4,3071]{3,2,1,0:T(4,128)}) fusion(f32[2,4,4,3072]{3,2,1,0:T(4,128)} %param.11), kind=kLoop, calls=%fused_computation.177 | loop fusion | bytes 1572352 | tf_op jit(solution)/shard_map/jit(_roll_static)/slice | solution.py:57
  18.2 0.1 fusion.94
  18.3 7.2 %fusion.35 = (f32[3072,128]{1,0:T(8,128)S(1)}, f32[3072,128]{1,0:T(8,128)}) fusion(), kind=kLoop, calls=%fused_computation.54 | loop fusion | flops 3538944 | bytes 3145728 | tf_op jit(solution)/shard_map/sin | solution.py:85
  25.5 0.1 broadcast_compare_fusion
  25.6 0.7 fusion.90
  26.3 0.3 slice.159
  27.3 0.0 slice-start
  27.3 0.0 copy-start.4
  27.3 0.2 maximum_convert_fusion
  27.6 0.2 slice_bitcast_fusion
  27.7 0.1 fusion.59
  27.8 0.1 fusion.61
  27.9 0.9 constant_dynamic-update-slice_fusion.1
  28.9 0.4 fusion.52
  29.3 0.1 slice.201
  29.4 0.2 fusion.46
  29.7 0.3 fusion.49
  30.0 7.4 %conditional.2 = (f32[2,4,4,3072]{3,2,1,0:T(4,128)S(1)}) conditional(s32[]{:T(128)} %convert_element_type.28, f32[2,4,4,3072]{3,2,1,0:T(4,128)S(1)} %fusion.49, (pred[4]{0:T(512)(128)(4,1)S(1)}, f32[2,4,4,3072]{3,2,1,0:T(4,128)S(1)}, f32[3072,128]{1,0:T(8,128)}, s32[4]{0:T(128)S(1)}, f32[3072,128]{1,0:T(8,128)}, /*index=5*/f32[3072,128]{1,0:T(8,128)S(1)}, ...), branch_computations={%region_1.2_spmd, %region_2.3_spmd} | conditional | flops 604186368 | bytes 15014968 | solution.py:112
  30.0 0.1 select_multiply_fusion
  30.1 2.6 %fusion.8 = f32[2,4,4,128]{3,2,1,0:T(4,128)S(1)} fusion(f32[2,4,4,3072]{3,2,1,0:T(4,128)S(1)} %get-tuple-element.82, f32[3072,128]{1,0:T(8,128)} %get-tuple-element.85, f32[4,128]{1,0:T(4,128)S(1)} %select_multiply_fusion), kind=kOutput, calls=%fused_computation.9 | convolution fusion | flops 150999040 | bytes 1984512 | tf_op jit(solution)/shard_map/cond/branch_1_fun/frln,nk->frlk/dot_general | solution.py:94
  32.7 1.7 %fusion.4 = f32[2,4,4,3072]{3,2,1,0:T(4,128)S(1)} fusion(f32[2,4,4,128]{3,2,1,0:T(4,128)S(1)} %fusion.8, f32[3072,128]{1,0:T(8,128)S(1)} %copy-done.1), kind=kOutput, calls=%fused_computation.5 | convolution fusion | flops 150994944 | bytes 1982464 | tf_op jit(solution)/shard_map/cond/branch_1_fun/frlk,nk->frln/dot_general | solution.py:104
  34.4 1.1 %fusion.11 = f32[2,4,4,128]{3,2,1,0:T(4,128)S(1)} fusion(f32[2,4,4,3072]{3,2,1,0:T(4,128)S(1)} %get-tuple-element.82, f32[3072,128]{1,0:T(8,128)S(1)} %get-tuple-element.87, f32[4,128]{1,0:T(4,128)S(1)} %select_multiply_fusion), kind=kOutput, calls=%fused_computation.10 | convolution fusion | flops 150999040 | bytes 1984512 | tf_op jit(solution)/shard_map/cond/branch_1_fun/frln,nk->frlk/dot_general | solution.py:97
  35.6 1.8 %fusion = f32[2,4,4,3072]{3,2,1,0:T(4,128)S(1)} fusion(f32[2,4,4,3072]{3,2,1,0:T(4,128)S(1)} %get-tuple-element.82, f32[2,4,4,3072]{3,2,1,0:T(4,128)S(1)} %fusion.4, f32[2,4,4,128]{3,2,1,0:T(4,128)S(1)} %fusion.11, f32[3072,128]{1,0:T(8,128)S(1)} %get-tuple-element.87, pred[4]{0:T(512)(128)(4,1)S(1)} %get-tuple-element.81), kind=kOutput, calls=%fused_computation.1 | convolution fusion | flops 151191552 | bytes 2768900 | tf_op jit(solution)/shard_map/cond/branch_1_fun/frlk,nk->frln/dot_general | solution.py:107
  37.4 0.3 fusion.92
  37.6 0.3 slice.215
  37.9 0.1 fusion.91
  38.0 4.0 %collective-permute-start.4 = (f32[2,2,4,3072]{3,2,1,0:T(4,128)S(1)}, f32[2,2,4,3072]{3,2,1,0:T(4,128)S(1)}, u32[]{:S(2)}, u32[]{:S(2)}) collective-permute-start(f32[2,2,4,3072]{3,2,1,0:T(4,128)S(1)} %get-tuple-element.119), channel_id=1, source_target_pairs={{0,16},{16,32},{32,48},{48,64},{64,80},{80,96},{96,112},{112,128},... | collective-permute-start | bytes 589832 | tf_op jit(solution)/shard_map/ppermute | solution.py:34
  42.0 1.3 %collective-permute-start.5 = (f32[2,2,4,3072]{3,2,1,0:T(4,128)S(1)}, f32[2,2,4,3072]{3,2,1,0:T(4,128)S(1)}, u32[]{:S(2)}, u32[]{:S(2)}) collective-permute-start(f32[2,2,4,3072]{3,2,1,0:T(4,128)S(1)} %get-tuple-element.120), channel_id=1, source_target_pairs={{16,0},{32,16},{48,32},{64,48},{80,64},{96,80},{112,96},{128,112},... | collective-permute-start | bytes 589832 | tf_op jit(solution)/shard_map/ppermute | solution.py:35
  43.3 0.4 fusion.56
  43.7 0.1 slice.217
  43.8 0.8 collective-permute-done.4
  44.6 5.6 %collective-permute-done.5 = f32[2,2,4,3072]{3,2,1,0:T(4,128)S(1)} collective-permute-done((f32[2,2,4,3072]{3,2,1,0:T(4,128)S(1)}, f32[2,2,4,3072]{3,2,1,0:T(4,128)S(1)}, u32[]{:S(2)}, u32[]{:S(2)}) %collective-permute-start.5) | collective-permute-done | bytes 196640 | tf_op jit(solution)/shard_map/ppermute | solution.py:35
  50.3 0.2 fusion.42
  50.5 0.3 fusion.48
  50.8 7.6 %conditional.3 = (f32[2,4,4,3072]{3,2,1,0:T(4,128)S(1)}) conditional(s32[]{:T(128)} %convert_element_type.28, f32[2,4,4,3072]{3,2,1,0:T(4,128)S(1)} %fusion.48, (pred[4]{0:T(512)(128)(4,1)S(1)}, f32[2,4,4,3072]{3,2,1,0:T(4,128)S(1)}, f32[3072,128]{1,0:T(8,128)}, s32[4]{0:T(128)S(1)}, f32[3072,128]{1,0:T(8,128)}, /*index=5*/f32[3072,128]{1,0:T(8,128)S(1)}, ...), branch_computations={%region_3.4_spmd, %region_4.5_spmd} | conditional | flops 604186368 | bytes 15014968 | solution.py:112
  51.0 0.1 select_multiply_fusion.1
  51.1 2.6 %fusion.22 = f32[2,4,4,128]{3,2,1,0:T(4,128)S(1)} fusion(f32[2,4,4,3072]{3,2,1,0:T(4,128)S(1)} %get-tuple-element.89, f32[3072,128]{1,0:T(8,128)} %get-tuple-element.92, f32[4,128]{1,0:T(4,128)S(1)} %select_multiply_fusion.1), kind=kOutput, calls=%fused_computation.23 | convolution fusion | flops 150999040 | bytes 1984512 | tf_op jit(solution)/shard_map/cond/branch_1_fun/frln,nk->frlk/dot_general | solution.py:94
  53.7 1.7 %fusion.18 = f32[2,4,4,3072]{3,2,1,0:T(4,128)S(1)} fusion(f32[2,4,4,128]{3,2,1,0:T(4,128)S(1)} %fusion.22, f32[3072,128]{1,0:T(8,128)S(1)} %copy-done.2), kind=kOutput, calls=%fused_computation.19 | convolution fusion | flops 150994944 | bytes 1982464 | tf_op jit(solution)/shard_map/cond/branch_1_fun/frlk,nk->frln/dot_general | solution.py:104
  55.4 1.1 %fusion.25 = f32[2,4,4,128]{3,2,1,0:T(4,128)S(1)} fusion(f32[2,4,4,3072]{3,2,1,0:T(4,128)S(1)} %get-tuple-element.89, f32[3072,128]{1,0:T(8,128)S(1)} %get-tuple-element.94, f32[4,128]{1,0:T(4,128)S(1)} %select_multiply_fusion.1), kind=kOutput, calls=%fused_computation.24 | convolution fusion | flops 150999040 | bytes 1984512 | tf_op jit(solution)/shard_map/cond/branch_1_fun/frln,nk->frlk/dot_general | solution.py:97
  56.6 1.8 %fusion.14 = f32[2,4,4,3072]{3,2,1,0:T(4,128)S(1)} fusion(f32[2,4,4,3072]{3,2,1,0:T(4,128)S(1)} %get-tuple-element.89, f32[2,4,4,3072]{3,2,1,0:T(4,128)S(1)} %fusion.18, f32[2,4,4,128]{3,2,1,0:T(4,128)S(1)} %fusion.25, f32[3072,128]{1,0:T(8,128)S(1)} %get-tuple-element.94, pred[4]{0:T(512)(128)(4,1)S(1)} %get-tuple-element.88), kind=kOutput, calls=%fused_computation.15 | convolution fusion | flops 151191552 | bytes 2768900 | tf_op jit(solution)/shard_map/cond/branch_1_fun/frlk,nk->frln/dot_general | solution.py:107
  58.4 0.1 slice_reduce_fusion
  58.5 22.4 %all-gather.1 = f32[16,4,3072]{2,1,0:T(4,128)S(1)} all-gather(f32[1,4,3072]{2,1,0:T(4,128)S(1)} %bitcast.130), channel_id=2, replica_groups=mesh['lat'=32,'lev'=16] {'lev'}, dimensions={0}, use_global_device_ids=true | all-gather | bytes 835584 | tf_op jit(solution)/shard_map/all_gather | solution.py:44
  80.9 0.8 while.12
  81.7 0.5 fusion.30
  82.2 0.1 bitcast_dynamic-update-slice_fusion.13
  82.3 0.1 bitcast_dynamic-update-slice_fusion.11
  82.4 0.1 bitcast_dynamic-update-slice_fusion.9
  82.6 0.1 bitcast_dynamic-update-slice_fusion.7
  82.7 0.1 bitcast_dynamic-update-slice_fusion.5
  82.8 0.1 bitcast_dynamic-update-slice_fusion.3
  83.0 0.1 bitcast_dynamic-update-slice_fusion.1
  83.1 0.1 fusion.80
  83.2 26.7 %all_to_all.5 = f32[16,3,4,4,192]{4,3,2,1,0:T(4,128)S(1)} all-to-all(f32[16,3,4,4,192]{4,3,2,1,0:T(4,128)S(1)} %fusion.80), channel_id=1, replica_groups=mesh['lat'=32,'lev'=16] {'lev'}, dimensions={0} | all-to-all | bytes 1179648 | tf_op jit(solution)/shard_map/all_to_all | solution.py:13
  110.0 0.2 slice.196
  110.2 0.8 squeeze.19
  111.0 1.4 %convolution_bitcast_fusion = f32[2,4,64,192]{3,2,1,0:T(8,128)} fusion(f32[2,4,64,192]{3,2,1,0:T(8,128)S(1)} %slice.196, f32[64,64]{1,0:T(8,128)S(1)} %copy-done), kind=kOutput, calls=%fused_computation.57 | convolution fusion | flops 75497472 | bytes 802816 | tf_op jit(solution)/shard_map/pk,fjkn->fjpn/dot_general | solution.py:154
  (52 shorter events, 0.8 us)
Async XLA Ops:
  0.6 110.4 %copy-start = (f32[64,64]{1,0:T(8,128)S(1)}, f32[64,64]{1,0:T(8,128)}, u32[]{:S(2)}) copy-start(f32[64,64]{1,0:T(8,128)} %param.15) | copy-start | bytes 49156
  0.6 17.6 %copy-start.3 = (f32[2,4,4,3072]{3,2,1,0:T(4,128)S(1)}, f32[2,4,4,3072]{3,2,1,0:T(4,128)}, u32[]{:S(2)}) copy-start(f32[2,4,4,3072]{3,2,1,0:T(4,128)} %param.11) | copy-start | bytes 1179652
  1.6 25.7 %collective-permute-start = (bf16[2,1,4,3072]{3,2,1,0:T(4,128)(2,1)S(1)}, bf16[2,1,4,3072]{3,2,1,0:T(4,128)(2,1)S(1)}, u32[]{:S(2)}, u32[]{:S(2)}) collective-permute-start(bf16[2,1,4,3072]{3,2,1,0:T(4,128)(2,1)S(1)} %get-tuple-element.130), channel_id=1, source_target_pairs={{0,16},{16,32},{32,48},{48,64},{64,80},{80,96},{96,112},{112,128},... | collective-permute-start | bytes 147464 | tf_op jit(solution)/shard_map/ppermute | solution.py:34
  6.4 20.9 %collective-permute-start.1 = (bf16[2,1,4,3072]{3,2,1,0:T(4,128)(2,1)S(1)}, bf16[2,1,4,3072]{3,2,1,0:T(4,128)(2,1)S(1)}, u32[]{:S(2)}, u32[]{:S(2)}) collective-permute-start(bf16[2,1,4,3072]{3,2,1,0:T(4,128)(2,1)S(1)} %get-tuple-element.131), channel_id=1, source_target_pairs={{16,0},{32,16},{48,32},{64,48},{80,64},{96,80},{112,96},{128,112},... | collective-permute-start | bytes 147464 | tf_op jit(solution)/shard_map/ppermute | solution.py:35
  9.5 18.4 %collective-permute-start.2 = (f32[2,2,4,3072]{3,2,1,0:T(4,128)}, f32[2,2,4,3072]{3,2,1,0:T(4,128)}, u32[]{:S(2)}, u32[]{:S(2)}) collective-permute-start(f32[2,2,4,3072]{3,2,1,0:T(4,128)} %get-tuple-element.128), channel_id=1, source_target_pairs={{0,16},{16,32},{32,48},{48,64},{64,80},{80,96},{96,112},{112,128},... | collective-permute-start | bytes 589832 | tf_op jit(solution)/shard_map/ppermute | solution.py:34
  14.8 14.6 %collective-permute-start.3 = (f32[2,2,4,3072]{3,2,1,0:T(4,128)}, f32[2,2,4,3072]{3,2,1,0:T(4,128)S(1)}, u32[]{:S(2)}, u32[]{:S(2)}) collective-permute-start(f32[2,2,4,3072]{3,2,1,0:T(4,128)} %get-tuple-element.129), channel_id=1, source_target_pairs={{16,0},{32,16},{48,32},{64,48},{80,64},{96,80},{112,96},{128,112},... | collective-permute-start | bytes 589832 | tf_op jit(solution)/shard_map/ppermute | solution.py:35
  18.3 7.2 %copy-start.7 = (s32[128]{0:T(128)S(1)}, s32[128]{0:T(128)}, u32[]{:S(2)}) copy-start(s32[128]{0:T(128)} %param.13) | copy-start | bytes 1540
  18.3 9.0 %copy-start.5 = (bf16[2,4,4,3072]{3,2,1,0:T(4,128)(2,1)S(1)}, bf16[2,4,4,3072]{3,2,1,0:T(4,128)(2,1)}, u32[]{:S(2)}) copy-start(bf16[2,4,4,3072]{3,2,1,0:T(4,128)(2,1)} %param.12) | copy-start | bytes 589828
  27.3 1.6 %slice-start = ((f32[2,4,4,3072]{3,2,1,0:T(4,128)}), f32[2,4,4,2]{3,2,1,0:T(4,128)S(1)}, s32[]{:S(2)}) async-start(f32[2,4,4,3072]{3,2,1,0:T(4,128)} %param.11), calls=%async_computation.1 | async-start | bytes 32768 | tf_op jit(solution)/shard_map/jit(_roll_static)/slice | solution.py:57
  27.3 1.6 %copy-start.4 = (f32[2,4,4,3071]{3,2,1,0:T(4,128)S(1)}, f32[2,4,4,3071]{3,2,1,0:T(4,128)}, u32[]{:S(2)}) copy-start(f32[2,4,4,3071]{3,2,1,0:T(4,128)} %get-tuple-element.127) | copy-start | bytes 1179268
  30.0 2.7 %copy-start.1 = (f32[3072,128]{1,0:T(8,128)S(1)}, f32[3072,128]{1,0:T(8,128)}, u32[]{:S(2)}) copy-start(f32[3072,128]{1,0:T(8,128)} %get-tuple-element.85) | copy-start | bytes 4718596 | tf_op jit(solution)/shard_map/cond
  38.0 6.6 %collective-permute-start.4 = (f32[2,2,4,3072]{3,2,1,0:T(4,128)S(1)}, f32[2,2,4,3072]{3,2,1,0:T(4,128)S(1)}, u32[]{:S(2)}, u32[]{:S(2)}) collective-permute-start(f32[2,2,4,3072]{3,2,1,0:T(4,128)S(1)} %get-tuple-element.119), channel_id=1, source_target_pairs={{0,16},{16,32},{32,48},{48,64},{64,80},{80,96},{96,112},{112,128},... | collective-permute-start | bytes 589832 | tf_op jit(solution)/shard_map/ppermute | solution.py:34
  42.0 8.2 %collective-permute-start.5 = (f32[2,2,4,3072]{3,2,1,0:T(4,128)S(1)}, f32[2,2,4,3072]{3,2,1,0:T(4,128)S(1)}, u32[]{:S(2)}, u32[]{:S(2)}) collective-permute-start(f32[2,2,4,3072]{3,2,1,0:T(4,128)S(1)} %get-tuple-element.120), channel_id=1, source_target_pairs={{16,0},{32,16},{48,32},{64,48},{80,64},{96,80},{112,96},{128,112},... | collective-permute-start | bytes 589832 | tf_op jit(solution)/shard_map/ppermute | solution.py:35
  51.0 2.7 %copy-start.2 = (f32[3072,128]{1,0:T(8,128)S(1)}, f32[3072,128]{1,0:T(8,128)}, u32[]{:S(2)}) copy-start(f32[3072,128]{1,0:T(8,128)} %get-tuple-element.92) | copy-start | bytes 4718596 | tf_op jit(solution)/shard_map/cond
  58.4 23.3 %copy-start.6 = (f32[4,3072]{1,0:T(4,128)S(1)}, f32[4,3072]{1,0:T(4,128)}, u32[]{:S(2)}) copy-start(f32[4,3072]{1,0:T(4,128)} %param.14) | copy-start | bytes 147460
